TPU v7x, 256 devices: a whole 4x4x8 slice. The times are simulated.
256 devices in a mesh: pop: 64 (over y, x_hi, z), merge: 4 (over x_lo, core).
Axes of the slice: x: 4 (x_hi: 2, x_lo: 2; x = x_hi * 2 + x_lo), y: 4, z: 8, core: 2. Of those that a mesh axis runs over, the one named last changes fastest.
Arguments:
- slab: float32 [256, 256, 4096], P('pop', 'merge'), may hold values from -6 to 6
- sample_counts: int32 [2], replicated, may hold values from 160 to 255
- mode_rows_one: float32 [96, 256], replicated, may hold values from -0.375 to 0.375
- mode_rows_two: float32 [96, 256], replicated, may hold values from -0.375 to 0.375
- merge_tensor: float32 [96, 96, 96], replicated, may hold values from -0.0625 to 0.0625
- ancestral_modes: float32 [96, 256], replicated, may hold values from -0.625 to 0.625
Outputs:
- merged: float32 [4096, 256], P(('pop', 'merge'))
All inputs are finite; a program needn't handle non-finite values.
Results may differ from a plain program's by a relative error of at most 0.000076.
Values sent between devices are 32-bit elements; how exact they have to be, the bound alone decides.
A program may use at most 64 MiB of HBM per device.

v0:
```python
import jax
import jax.numpy as jnp
from jax import lax
from jax.sharding import PartitionSpec as P

branch_one = 0.00025
branch_two = 0.0004


def split_up(value, dim, length):
    lengths = value.shape
    blocks = value.reshape(*lengths[:dim], length, lengths[dim] // length, *lengths[dim + 1 :])
    return jnp.moveaxis(blocks, dim, 0)


def summed_on_arrival(value, axis, dim):
    blocks = split_up(value, dim, lax.axis_size(axis))
    arrived = lax.all_to_all(blocks, axis, split_axis=0, concat_axis=0, tiled=True)
    return arrived.sum(axis=0)


def prepared(rows, count, branch):
    order = jnp.arange(rows.shape[0], dtype=jnp.float32)
    decay = jnp.exp(-branch * order * (order + 1.0) / 2.0)
    keep = jnp.arange(rows.shape[1], dtype=jnp.int32) <= count
    return jnp.where(keep[None, :], rows, jnp.zeros_like(rows)) * decay[:, None]


def on_device(slab, sample_counts, mode_rows_one, mode_rows_two, merge_tensor, ancestral_modes):
    high = lax.Precision.HIGHEST
    modes = mode_rows_one.shape[0]
    proj_one = prepared(mode_rows_one, sample_counts[0], branch_one)
    proj_two = prepared(mode_rows_two, sample_counts[1], branch_two)
    merge_count = lax.axis_size("merge")
    per_merge = mode_rows_two.shape[1] // merge_count
    modal = jnp.einsum(
        "ka,abc->kbc",
        proj_one,
        lax.all_to_all(slab, "pop", split_axis=1, concat_axis=0, tiled=True),
        precision=high,
    )
    regrouped = lax.all_to_all(modal, "pop", split_axis=2, concat_axis=1, tiled=True)
    begin_col = lax.axis_index("merge") * per_merge
    folded = jnp.einsum(
        "mnj,nb->jmb",
        merge_tensor,
        lax.dynamic_slice_in_dim(proj_two, begin_col, per_merge, 1),
        precision=high,
    ).reshape(modes, -1)
    stacked = regrouped.reshape(modes * per_merge, -1)
    summed = summed_on_arrival(
        lax.dot_general(stacked, folded, (((0,), (1,)), ((), ())), precision=high), "merge", 0
    )
    return jnp.dot(summed, ancestral_modes, precision=high)


def solution(mesh):
    in_specs = (P("pop", "merge", None), P(), P(), P(), P(), P())
    out_specs = P(("pop", "merge"), None)
    return jax.shard_map(
        on_device, mesh=mesh, in_specs=in_specs, out_specs=out_specs, check_vma=False
    )
```

profile of v0, /device:TPU:1, one launch (start us, length us, event | category | flops | bytes accessed | tf_op | source)
XLA Modules:
  0.0 217.5 jit_solution(16682954837611446989)
XLA Ops:
  0.0 0.0 copy-start
  0.0 6.9 %copy.14 = f32[4,64,4096]{2,0,1:T(4,128)} copy(f32[4,64,4096]{2,1,0:T(8,128)} %param.6) | data formatting | bytes 8388608 | tf_op args[0]
  6.9 0.0 copy-start.1
  6.9 0.0 copy-start.3
  6.9 15.5 %all-to-all-start = ((f32[4,64,4096]{2,0,1:T(4,128)}), f32[4,64,4096]{2,0,1:T(4,128)}, u32[]{:S(2)}, u32[]{:S(2)}) async-start(f32[4,64,4096]{2,0,1:T(4,128)} %copy.14), calls=%async_computation | async-start | bytes 8388608 | tf_op jit(solution)/shard_map/all_to_all | solution.py:39
  22.4 0.0 copy-done.1
  22.4 0.1 copy.13
  22.5 0.0 copy-done.3
  22.5 0.6 fusion.21
  23.1 0.6 iota_compare_fusion.1
  23.8 91.6 %all-to-all-done = f32[4,64,4096]{2,0,1:T(4,128)} async-done(((f32[4,64,4096]{2,0,1:T(4,128)}), f32[4,64,4096]{2,0,1:T(4,128)}, u32[]{:S(2)}, u32[]{:S(2)}) %all-to-all-start) | async-done | bytes 4194336 | tf_op jit(solution)/shard_map/all_to_all | solution.py:39
  115.3 5.3 %reshape.43 = f32[256,4096]{1,0:T(8,128)} reshape(f32[64,4,1,4096]{3,1,0,2:T(4,128)} %bitcast.2) | data formatting | bytes 8388608 | tf_op jit(solution)/shard_map/reshape
  120.7 10.2 %fusion = f32[96,4096]{0,1:T(8,128)} fusion(f32[256,4096]{1,0:T(8,128)} %reshape.43, f32[96,256]{0,1:T(8,128)S(1)} %copy.13, f32[96]{0:T(128)S(1)} %fusion.16, pred[256]{0:T(512)(128)(4,1)S(1)} %iota_compare_fusion.1), kind=kOutput, calls=%fused_computation | convolution fusion | flops 1208008704 | bytes 5866112 | tf_op jit(solution)/shard_map/ka,abc->kbc/dot_general | solution.py:36
  130.9 11.2 %all-to-all-start.1 = ((f32[96,1,4096]{0,1,2:T(1,128)}), f32[96,1,4096]{0,1,2:T(1,128)}, u32[]{:S(2)}, u32[]{:S(2)}) async-start(f32[96,1,4096]{0,1,2:T(1,128)} %bitcast.14), calls=%async_computation.1 | async-start | bytes 4194304 | tf_op jit(solution)/shard_map/all_to_all | solution.py:42
  142.1 0.0 copy-done
  142.1 0.1 constant_dynamic-slice_fusion
  142.2 0.1 copy.22
  142.2 0.7 iota_compare_fusion
  142.9 0.1 dynamic-slice
  143.0 4.6 %fusion.6 = f32[64,96,96]{2,0,1:T(8,128)S(1)} fusion(f32[96,96,96]{2,1,0:T(8,128)} %param.10, f32[96,64]{0,1:T(8,128)S(1)} %copy.22, f32[96]{0:T(128)S(1)} %fusion.18, pred[64]{0:T(512)(128)(4,1)S(1)} %dynamic-slice), kind=kOutput, calls=%fused_computation.6 | convolution fusion | flops 679489536 | bytes 5923264 | tf_op jit(solution)/shard_map/mnj,nb->jmb/dot_general | solution.py:44
  147.7 43.2 %all-to-all-done.1 = f32[96,1,4096]{0,1,2:T(1,128)} async-done(((f32[96,1,4096]{0,1,2:T(1,128)}), f32[96,1,4096]{0,1,2:T(1,128)}, u32[]{:S(2)}, u32[]{:S(2)}) %all-to-all-start.1) | async-done | bytes 1572896 | tf_op jit(solution)/shard_map/all_to_all | solution.py:42
  190.8 5.4 %copy.16 = f32[96,1,4096]{2,0,1:T(8,128)} copy(f32[96,1,4096]{0,1,2:T(1,128)} %all-to-all-done.1) | data formatting | bytes 3145728 | tf_op jit(solution)/shard_map/all_to_all | solution.py:42
  196.2 3.6 %reshape.44 = f32[6144,64]{1,0:T(8,128)} reshape(f32[96,1,4096]{2,0,1:T(8,128)} %copy.16) | data formatting | bytes 3145728 | tf_op jit(solution)/shard_map/reshape | solution.py:50
  199.8 3.2 %copy.17 = f32[64,6144]{1,0:T(8,128)} copy(f32[64,6144]{0,1:T(8,128)} %bitcast.28) | data formatting | bytes 3145728 | tf_op jit(solution)/shard_map/dot_general | solution.py:52
  203.0 0.0 copy-start.2
  203.0 3.5 %fusion.22 = f32[4,16,96]{2,1,0:T(8,128)S(1)} fusion(f32[4,16,6144]{2,1,0:T(8,128)} %bitcast.29, f32[96,6144,1]{0,1,2:T(8,128)S(1)} %bitcast.27), kind=kOutput, calls=%fused_computation.27 | convolution fusion | flops 452984832 | bytes 3956736 | tf_op jit(solution)/shard_map/dot_general | solution.py:52
  206.5 10.2 %all_to_all.29 = f32[4,16,96]{2,1,0:T(8,128)S(1)} all-to-all(f32[4,16,96]{2,1,0:T(8,128)S(1)} %fusion.22), channel_id=1, replica_groups=mesh['pop'=64,'merge'=4] {'merge'}, dimensions={0} | all-to-all | bytes 49152 | tf_op jit(solution)/shard_map/all_to_all | solution.py:18
  216.7 0.0 copy-done.2
  216.7 0.8 fusion.23
  (3 shorter events, 0.0 us)
Async XLA Ops:
  0.0 142.1 %copy-start = (f32[96,256]{1,0:T(8,128)S(1)}, f32[96,256]{1,0:T(8,128)}, u32[]{:S(2)}) copy-start(f32[96,256]{1,0:T(8,128)} %param.9) | copy-start | bytes 294916
  6.9 15.5 %copy-start.1 = (f32[96,256]{1,0:T(8,128)S(1)}, f32[96,256]{1,0:T(8,128)}, u32[]{:S(2)}) copy-start(f32[96,256]{1,0:T(8,128)} %param.8) | copy-start | bytes 294916
  6.9 15.6 %copy-start.3 = (s32[2]{0:T(128)S(1)}, s32[2]{0:T(128)}, u32[]{:S(2)}) copy-start(s32[2]{0:T(128)} %param.7) | copy-start | bytes 28
  6.9 108.4 %all-to-all-start = ((f32[4,64,4096]{2,0,1:T(4,128)}), f32[4,64,4096]{2,0,1:T(4,128)}, u32[]{:S(2)}, u32[]{:S(2)}) async-start(f32[4,64,4096]{2,0,1:T(4,128)} %copy.14), calls=%async_computation | async-start | bytes 8388608 | tf_op jit(solution)/shard_map/all_to_all | solution.py:39
  130.9 59.9 %all-to-all-start.1 = ((f32[96,1,4096]{0,1,2:T(1,128)}), f32[96,1,4096]{0,1,2:T(1,128)}, u32[]{:S(2)}, u32[]{:S(2)}) async-start(f32[96,1,4096]{0,1,2:T(1,128)} %bitcast.14), calls=%async_computation.1 | async-start | bytes 4194304 | tf_op jit(solution)/shard_map/all_to_all | solution.py:42
  203.0 13.7 %copy-start.2 = (f32[96,256]{1,0:T(8,128)S(1)}, f32[96,256]{1,0:T(8,128)}, u32[]{:S(2)}) copy-start(f32[96,256]{1,0:T(8,128)} %param.11) | copy-start | bytes 294916
where the time goes:
time: 218 us
  waiting for transfers between devices  135 us (62%)
  starting transfers between devices  26.7 us (12%)
  local copies, waits for them, and re-layouts  25.3 us (12%)
  matrix products  19.1 us (9%)
  blocking collectives  10.2 us (5%)
    all_to_all x1, waiting for transfers between devices, on_device(): lax.all_to_all(slab, 'pop', split_axis=1, concat_axis=0, tiled=True)  91.6 us
    all_to_all x1, waiting for transfers between devices, on_device(): lax.all_to_all(modal, 'pop', split_axis=2, concat_axis=1, tiled=True)  43.2 us
    all_to_all x1, starting transfers between devices, on_device(): lax.all_to_all(slab, 'pop', split_axis=1, concat_axis=0, tiled=True)  15.5 us
    all_to_all x1, starting transfers between devices, on_device(): lax.all_to_all(modal, 'pop', split_axis=2, concat_axis=1, tiled=True)  11.2 us
    dot_general x1, matrix products, on_device(): jnp.einsum('ka,abc->kbc', proj_one, lax.all_to_all(slab, 'pop', split_axi...  10.2 us
    all_to_all x1, blocking collectives, summed_on_arrival(): lax.all_to_all(blocks, axis, split_axis=0, concat_axis=0, tiled=True)  10.2 us
    unnamed x11, local copies, waits for them, and re-layouts  7.06 us
    all_to_all x1, local copies, waits for them, and re-layouts, on_device(): lax.all_to_all(modal, 'pop', split_axis=2, concat_axis=1, tiled=True)  5.43 us
  transfers between devices with their start and end apart: 2, of which 2 were waited for; matrix products, arithmetic and copies ran while one was open for 3% of the time, Pallas kernels for 0%

commit v1 on v0

v1 whole, which is shorter than its diff:
```python
import jax
import jax.numpy as jnp
from jax import lax
from jax.sharding import PartitionSpec as P

branch_one = 0.00025
branch_two = 0.0004


def prepared(rows, first, count, branch):
    order = jnp.arange(rows.shape[0], dtype=jnp.float32)
    decay = jnp.exp(-branch * order * (order + 1.0) / 2.0)
    keep = first + jnp.arange(rows.shape[1], dtype=jnp.int32) <= count
    return jnp.where(keep[None, :], rows, jnp.zeros_like(rows)) * decay[:, None]


def on_device(slab, sample_counts, mode_rows_one, mode_rows_two, merge_tensor, ancestral_modes):
    high = lax.Precision.HIGHEST
    per_pop, per_merge, cols = slab.shape
    begin_one = lax.axis_index("pop") * per_pop
    begin_two = lax.axis_index("merge") * per_merge
    rows_one = lax.dynamic_slice_in_dim(mode_rows_one, begin_one, per_pop, 1)
    rows_two = lax.dynamic_slice_in_dim(mode_rows_two, begin_two, per_merge, 1)
    proj_one = prepared(rows_one, begin_one, sample_counts[0], branch_one)
    proj_two = prepared(rows_two, begin_two, sample_counts[1], branch_two)
    half = jnp.einsum("ma,mnj->anj", proj_one, merge_tensor, precision=high)
    weights = jnp.einsum("nb,anj->abj", proj_two, half, precision=high)
    partial = lax.dot_general(
        slab, weights, (((0, 1), (0, 1)), ((), ())), precision=lax.Precision.HIGH
    )
    summed = lax.psum_scatter(partial, ("pop", "merge"), scatter_dimension=0, tiled=True)
    return jnp.dot(summed, ancestral_modes, precision=high)


def solution(mesh):
    in_specs = (P("pop", "merge", None), P(), P(), P(), P(), P())
    out_specs = P(("pop", "merge"), None)
    return jax.shard_map(
        on_device, mesh=mesh, in_specs=in_specs, out_specs=out_specs, check_vma=False
    )
```

time: 218 us -> 1300 us (5.96)
  waiting for transfers between devices: 135 us -> 1270 us
  starting transfers between devices: 26.7 us -> 0.01 us
  local copies, waits for them, and re-layouts: 25.3 us -> 3.16 us
  between operations: 0.1 us -> 13.4 us
    unnamed x0 -> x2, waiting for transfers between devices: none -> 1270 us
    all_to_all x2 -> x0, waiting for transfers between devices: 135 us -> none  [the longest x1 91.6 us: on_device(): lax.all_to_all(slab, 'pop', split_axis=1, concat_axis=0, tiled=True)]
    all_to_all x2 -> x0, starting transfers between devices: 26.7 us -> none  [the longest x1 15.5 us: on_device(): lax.all_to_all(slab, 'pop', split_axis=1, concat_axis=0, tiled=True)]
  transfers between devices with their start and end apart: 2 -> 1, of which waited for: 2 -> 1; matrix products, arithmetic and copies ran while one was open for 3% -> 0% of each run, Pallas kernels for 0% -> 0%
where the time goes in v1:
time: 1300 us
  waiting for transfers between devices  1270 us (98%)
  between operations  13.4 us (1%)
    unnamed x2, waiting for transfers between devices  1270 us
  transfers between devices with their start and end apart: 1, of which 1 were waited for; matrix products, arithmetic and copies ran while one was open for 0% of the time, Pallas kernels for 0%

profile of v1, /device:TPU:1, one launch (start us, length us, event | category | flops | bytes accessed | tf_op | source)
XLA Modules:
  0.0 1299.2 jit_solution(16404460061027357766)
XLA Ops:
  6.5 0.0 copy-start
  6.5 0.0 copy-start.2
  6.5 0.0 reduce-scatter.4.cloned.1.call-start
  6.6 1.3 fusion.27
  7.9 0.7 add_compare_fusion
  8.5 0.6 add_compare_fusion.1
  9.2 0.0 copy-start.1
  9.2 7.3 fusion
  16.5 0.0 copy-done.2
  16.5 0.5 convolution_bitcast_fusion.1
  17.0 0.0 copy-done.1
  17.1 1.5 convolution_bitcast_fusion
  18.6 1.8 copy.9
  20.4 0.0 reduce-scatter.4.cloned.1.call-update
  20.5 1270.4 %reduce-scatter.4.cloned.1.call-done = f32[16,96]{1,0:T(8,128)} async-done(((f32[4096,96]{1,0:T(8,128)}), f32[16,96]{1,0:T(8,128)}) %reduce-scatter.4.cloned.1.call-update) | async-done | bytes 6160
  1290.8 0.0 copy-done
  1290.8 1.5 fusion.28
  (2 shorter events, 0.0 us)
Async XLA Ops:
  6.5 1284.3 %copy-start = (f32[96,256]{1,0:T(8,128)S(1)}, f32[96,256]{1,0:T(8,128)}, u32[]{:S(2)}) copy-start(f32[96,256]{1,0:T(8,128)} %param.11) | copy-start | bytes 294916
  6.5 10.0 copy-start.2
  6.5 1284.3 %reduce-scatter.4.cloned.1.call-start = ((), (), s32[]{:S(2)}) async-start(), calls=%async_computation.1 | async-start | bytes 2105344
  9.2 7.9 copy-start.1
Sparse Core Ops, SparseCore 0:
  20.6 1270.2 reduce-scatter.3

commit v2 on v1

v2 whole, which is shorter than its diff:
```python
import jax
import jax.numpy as jnp
from jax import lax
from jax.experimental import pallas as pl
from jax.experimental.pallas import tpu as pltpu
from jax.sharding import PartitionSpec as P

branch_one = 0.00025
branch_two = 0.0004
MESH = pl.DeviceIdType.MESH
HIGH = lax.Precision.HIGHEST
LAG = 4
F32 = jnp.float32


def device(y, xh, z, xl, c):
    return ((y * 2 + xh) * 8 + z, xl * 2 + c)


def flip(bit, by):
    return (bit + by) % 2


def prepared(rows, count, branch):
    order = lax.broadcasted_iota(jnp.int32, rows.shape, 0).astype(F32)
    entry = lax.broadcasted_iota(jnp.int32, rows.shape, 1)
    decay = jnp.exp(-branch * order * (order + 1.0) / 2.0)
    return jnp.where(entry <= count, rows, 0.0) * decay


def kernel(
    slab, counts, rows_one, rows_two, merge, ancestral, out,
    slab_v, one_v, two_v, merge_v, anc_v, anc_pad, one_b, half_v, weights, whi, part, from_core,
    arrived_y, arrived_x, tiles_out, pieces,
    load_sem, slab_sem, merge_sem, core_send, core_recv, y_send, y_recv, x_send, x_recv,
    final_send, final_recv,
):
    pop, mrg = lax.axis_index("pop"), lax.axis_index("merge")
    z = pop % 8
    xh = (pop // 8) % 2
    y = pop // 16
    xl, c = mrg // 2, mrg % 2
    yh, yl = y // 2, y % 2
    zh, zl = z // 2, z % 2
    low = 1 - z // 4

    def y_target(i):
        k = (i % 4 + 1) % 4
        return k, flip(yh, k // 2) * 2 + flip(yl, k % 2), flip(xh, 1 - i // 4)

    def x_target(i):
        k = i % 4
        xr = 1 - k % 2
        u = (i // 4) * 2 + k // 2
        return u, flip(yh, 1 - i // 4) * 2 + flip(yl, k // 2), xr

    def slab_copy(i, h):
        if h == 0:
            _, ty, tx = y_target(i)
            pair = ty * 4 + tx * 2
        else:
            _, ty, xr = x_target(i)
            pair = ty * 4 + flip(xh, xr) * 2 + 1
        begin = pl.multiple_of(pair * 256, 256)
        return pltpu.make_async_copy(
            slab.at[:, :, pl.ds(begin, 256)], slab_v.at[i, h], slab_sem.at[i, h]
        )

    load_one = pltpu.make_async_copy(rows_one, one_v, load_sem.at[0])
    load_two = pltpu.make_async_copy(rows_two, two_v, load_sem.at[1])
    load_anc = pltpu.make_async_copy(ancestral, anc_v, load_sem.at[2])
    load_one.start()
    load_two.start()
    merge_loads = [
        pltpu.make_async_copy(
            merge.at[:, pl.ds(b * 4, 4)], merge_v.at[:, pl.ds(b * 4, 4)], merge_sem.at[b]
        )
        for b in range(3)
    ]
    for load in merge_loads:
        load.start()

    def start_slab(i, _):
        slab_copy(i, 0).start()
        slab_copy(i, 1).start()
        return 0

    lax.fori_loop(0, 8, start_slab, 0)
    load_anc.start()

    barrier = pltpu.get_barrier_semaphore()

    def tell(dev):
        pl.semaphore_signal(barrier, inc=1, device_id=dev, device_id_type=MESH)

    tell(device(y, xh, z, xl, 1 - c))
    for k in range(1, 4):
        tell(device(flip(yh, k // 2) * 2 + flip(yl, k % 2), xh, z, xl, c))
        tell(device(y, flip(xh, k // 2), z, flip(xl, k % 2), c))

    def tell_sources(i, _):
        n, zs = i // 8, i % 8
        ys = low * y + (1 - low) * n
        xhs = low * (n // 2) + (1 - low) * xh
        xls = low * (n % 2) + (1 - low) * (zh - 2)
        me = (ys == y) & (xhs == xh) & (xls == xl) & (zs == z)

        @pl.when(jnp.logical_not(me))
        def _():
            tell(device(ys, xhs, zs, xls, c))

        return 0

    lax.fori_loop(0, 32, tell_sources, 0)
    own_piece = (low == 1) | (zh == 2 + xl)

    load_one.wait()
    load_two.wait()
    one = prepared(one_v[...], counts[0], branch_one)
    entry = lax.broadcasted_iota(jnp.int32, one.shape, 1)
    for a in range(4):
        column = jnp.sum(jnp.where(entry == pop * 4 + a, one, 0.0), axis=1, keepdims=True)
        one_b[a] = jnp.broadcast_to(column[:, :, None], (96, 8, 96))
    two = prepared(two_v[...], counts[1], branch_two)
    two = pltpu.roll(two, (256 - mrg * 64) % 256, 1)
    two_t = jnp.transpose(two[:, :128])[:64]
    half_v[...] = jnp.zeros_like(half_v)
    for b in range(3):
        merge_loads[b].wait()

        def mode_step(mb, acc):
            for s in range(8):
                m = mb * 8 + s
                block = merge_v[m, b * 4 : b * 4 + 4]
                acc = tuple(acc[a] + one_b[a, m][None] * block for a in range(4))
            return acc

        acc = lax.fori_loop(0, 12, mode_step, tuple(jnp.zeros((4, 8, 96), F32) for _ in range(4)))
        for a in range(4):
            half_v[b * 32 : b * 32 + 32, a * 128 : a * 128 + 96] = acc[a].reshape(32, 96)
    wide = jnp.dot(two_t, half_v[...], precision=HIGH, preferred_element_type=F32)
    flat = jnp.concatenate([wide[:, a * 128 : a * 128 + 128] for a in range(4)], axis=0)
    w = jnp.transpose(flat)[:96]
    w_hi = w.astype(jnp.bfloat16)
    weights[:96] = w_hi
    weights[96:] = (w - w_hi.astype(F32)).astype(jnp.bfloat16)
    whi[...] = w_hi

    pl.semaphore_wait(barrier, jnp.where(own_piece, 38, 39))

    def core_copy(i, h):
        return pltpu.make_async_remote_copy(
            src_ref=part.at[i, h, 1 - c],
            dst_ref=from_core.at[i, h],
            send_sem=core_send,
            recv_sem=core_recv.at[i, h],
            device_id=device(y, xh, z, xl, 1 - c),
            device_id_type=MESH,
        )

    def contract(i, h):
        slab_copy(i, h).wait()
        x = slab_v[i, h].reshape(256, 256)
        x_hi = x.astype(jnp.bfloat16)
        x_lo = (x - x_hi.astype(F32)).astype(jnp.bfloat16)
        both = jnp.dot(weights[...], x_hi, preferred_element_type=F32)
        rest = jnp.dot(whi[...], x_lo, preferred_element_type=F32)
        total = both[:96] + both[96:] + rest
        for j in range(2):
            for t in range(2):
                part[i, h, j, t] = total[j * 48 : j * 48 + 48, t * 128 : t * 128 + 128]
        core_copy(i, h).start()

    def forward(i):
        k, ty, _ = y_target(i)
        core_copy(i, 0).wait_recv()
        part[i, 0, c] = part[i, 0, c] + from_core[i, 0]

        @pl.when(k > 0)
        def _():
            pltpu.make_async_remote_copy(
                src_ref=part.at[i, 0, c],
                dst_ref=arrived_y.at[k - 1, i // 4],
                send_sem=y_send,
                recv_sem=y_recv.at[k - 1, i // 4],
                device_id=device(ty, xh, z, xl, c),
                device_id_type=MESH,
            ).start()

        u, _, xr = x_target(i)
        core_copy(i, 1).wait_recv()
        part[i, 1, c] = part[i, 1, c] + from_core[i, 1]

        def send_x(tr):
            t = flip(xl, tr)
            pltpu.make_async_remote_copy(
                src_ref=part.at[i, 1, c, t],
                dst_ref=arrived_x.at[xr * 2 + tr - 1, u],
                send_sem=x_send,
                recv_sem=x_recv.at[xr * 2 + tr - 1, u],
                device_id=device(y, flip(xh, xr), z, t, c),
                device_id_type=MESH,
            ).start()

        send_x(1)

        @pl.when(xr == 1)
        def _():
            send_x(0)

    def step(i, _):
        @pl.when(i < 8)
        def _():
            contract(i, 0)
            contract(i, 1)

        @pl.when(i >= LAG)
        def _():
            forward(i - LAG)

        return 0

    lax.fori_loop(0, 8 + LAG, step, 0)

    load_anc.wait()
    anc_pad[...] = jnp.zeros_like(anc_pad)
    anc_pad[0:48] = anc_v[0:48]
    anc_pad[64:112] = anc_v[48:96]

    def spread(total, n, h):
        zero = jnp.zeros((16, 128), F32)
        stacked = jnp.concatenate([total, zero, pltpu.roll(total, 120, 1), zero], axis=0)
        turned = jnp.transpose(stacked)
        for g in range(8):
            tiles_out[h, n, g] = turned[g * 16 : g * 16 + 8]

    def final_copy(n, h, g, slot, dev):
        return pltpu.make_async_remote_copy(
            src_ref=tiles_out.at[h, n, g],
            dst_ref=pieces.at[slot],
            send_sem=final_send,
            recv_sem=final_recv,
            device_id=dev,
            device_id_type=MESH,
        )

    def owner_step(n, _):
        q, t = n // 2, n % 2
        @pl.when(t == 0)
        def _():
            for k in range(3):
                pltpu.make_async_copy(
                    arrived_y.at[k, q], arrived_y.at[k, q], y_recv.at[k, q]
                ).wait()

        mine = part[q * 4 + 3, 0, c, t]
        spread(mine + arrived_y[0, q, t] + arrived_y[1, q, t] + arrived_y[2, q, t], n, 0)
        slot = (xh * 2 + xl) * 16 + z * 2 + c
        for r in range(8):
            gz, gx, gc = flip(zl, r // 4), flip(xl, r // 2 % 2), flip(c, r % 2)
            g = gz * 4 + gx * 2 + gc
            dev = device(y, flip(xh, 1 - q), t * 2 + gz, gx, gc)
            if r == 0:
                own = (q == 1) & (zh == t)

                @pl.when(own)
                def _():
                    pieces[slot] = tiles_out[0, n, g]

                @pl.when(jnp.logical_not(own))
                def _():
                    final_copy(n, 0, g, slot, dev).start()
            else:
                final_copy(n, 0, g, slot, dev).start()

        for k in range(3):
            pltpu.make_async_copy(
                arrived_x.at[k, n], arrived_x.at[k, n], x_recv.at[k, n]
            ).wait()
        mine = part[q * 4 + t * 2 + 1, 1, c, xl]
        spread(mine + arrived_x[0, n] + arrived_x[1, n] + arrived_x[2, n], n, 1)
        slot = y * 16 + z * 2 + c
        ty = flip(yh, 1 - q) * 2 + flip(yl, t)
        for r in range(8):
            gz, gx, gc = flip(zl, r // 4), flip(xl, r // 2 % 2), flip(c, r % 2)
            g = gz * 4 + gx * 2 + gc
            dev = device(ty, xh, (2 + xl) * 2 + gz, gx, gc)
            if r == 0:
                own = (n == 2) & (zh == 2 + xl)

                @pl.when(own)
                def _():
                    pieces[slot] = tiles_out[1, n, g]

                @pl.when(jnp.logical_not(own))
                def _():
                    final_copy(n, 1, g, slot, dev).start()
            else:
                final_copy(n, 1, g, slot, dev).start()
        return 0

    lax.fori_loop(0, 4, owner_step, 0)

    def drain(ref, sem):
        pltpu.make_async_copy(ref, ref, sem).wait()

    def drain_pieces(sem):
        @pl.when(own_piece)
        def _():
            drain(pieces.at[pl.ds(0, 63)], sem)

        @pl.when(jnp.logical_not(own_piece))
        def _():
            drain(pieces, sem)

    drain_pieces(final_recv)

    def add(i, acc):
        return acc[0] + pieces[i * 2], acc[1] + pieces[i * 2 + 1]

    first, second = lax.fori_loop(1, 32, add, (pieces[0], pieces[1]), unroll=True)
    lane = lax.broadcasted_iota(jnp.int32, (8, 128), 1)
    top = jnp.where(lane < 64, first, pltpu.roll(second, 64, 1))
    bottom = jnp.where(lane < 64, pltpu.roll(first, 64, 1), second)
    out[...] = jnp.dot(
        jnp.concatenate([top, bottom], axis=0), anc_pad[...],
        precision=HIGH, preferred_element_type=F32,
    )

    drain(from_core, core_send)
    drain(arrived_y, y_send)
    drain(arrived_x, x_send)
    drain_pieces(final_send)


def on_device(slab, sample_counts, mode_rows_one, mode_rows_two, merge_tensor, ancestral_modes):
    hbm = pl.BlockSpec(memory_space=pl.ANY)
    dma = pltpu.SemaphoreType.DMA
    return pl.pallas_call(
        kernel,
        out_shape=jax.ShapeDtypeStruct((16, 256), F32),
        in_specs=[hbm, pl.BlockSpec(memory_space=pltpu.SMEM), hbm, hbm, hbm, hbm],
        out_specs=pl.BlockSpec(memory_space=pltpu.VMEM),
        scratch_shapes=[
            pltpu.VMEM((8, 2, 4, 64, 256), F32),
            pltpu.VMEM((96, 256), F32),
            pltpu.VMEM((96, 256), F32),
            pltpu.VMEM((96, 12, 8, 96), F32),
            pltpu.VMEM((96, 256), F32),
            pltpu.VMEM((128, 256), F32),
            pltpu.VMEM((4, 96, 8, 96), F32),
            pltpu.VMEM((96, 512), F32),
            pltpu.VMEM((192, 256), jnp.bfloat16),
            pltpu.VMEM((96, 256), jnp.bfloat16),
            pltpu.VMEM((8, 2, 2, 2, 48, 128), F32),
            pltpu.VMEM((8, 2, 2, 48, 128), F32),
            pltpu.VMEM((3, 2, 2, 48, 128), F32),
            pltpu.VMEM((3, 4, 48, 128), F32),
            pltpu.VMEM((2, 4, 8, 8, 128), F32),
            pltpu.VMEM((64, 8, 128), F32),
            dma((3,)),
            dma((8, 2)),
            dma((3,)),
            dma,
            dma((8, 2)),
            dma,
            dma((3, 2)),
            dma,
            dma((3, 4)),
            dma,
            dma,
        ],
        compiler_params=pltpu.CompilerParams(
            collective_id=0, has_side_effects=True, vmem_limit_bytes=56 << 20
        ),
    )(
        slab,
        sample_counts,
        mode_rows_one,
        mode_rows_two,
        merge_tensor.reshape(96, 12, 8, 96),
        ancestral_modes,
    )


def solution(mesh):
    in_specs = (P("pop", "merge", None), P(), P(), P(), P(), P())
    out_specs = P(("pop", "merge"), None)
    return jax.shard_map(
        on_device, mesh=mesh, in_specs=in_specs, out_specs=out_specs, check_vma=False
    )
```

time: 1300 us -> 34.5 us (0.03)
  waiting for transfers between devices: 1270 us -> 0 us
  Pallas kernels: 0 us -> 33 us
  between operations: 13.4 us -> 0.01 us
    unnamed x2 -> x0, waiting for transfers between devices: 1270 us -> none
    pallas_call x0 -> x1, Pallas kernels: none -> 33 us  [on_device(): pl.pallas_call(kernel, out_shape=jax.ShapeDtypeStruct((16, 256), F32), in...]
  transfers between devices with their start and end apart: 1 -> 0, of which waited for: 1 -> 0; matrix products, arithmetic and copies ran while one was open for 0% -> 0% of each run, Pallas kernels for 0% -> 0%
where the time goes in v2:
time: 34.5 us; the launch traced here: 34.3 us
  Pallas kernels  33 us (96%)
  local copies, waits for them, and re-layouts  1.32 us (4%)
    pallas_call x1, Pallas kernels, on_device(): pl.pallas_call(kernel, out_shape=jax.ShapeDtypeStruct((16, 256), F32), in...  33 us
    unnamed x1, local copies, waits for them, and re-layouts  1.32 us

profile of v2, /device:TPU:1, one launch (start us, length us, event | category | flops | bytes accessed | tf_op | source)
XLA Modules:
  0.0 34.3 jit_solution(17570040293761878692)
XLA Ops:
  0.0 33.0 %shard_map.64 = f32[16,256]{1,0:T(8,128)} custom-call(f32[4,64,4096]{2,1,0:T(8,128)} %slab.1, s32[2]{0:T(128)} %counts.1, f32[96,256]{1,0:T(8,128)} %rows_one.1, f32[96,256]{1,0:T(8,128)} %rows_two.1, f32[96,12,8,96]{3,2,1,0:T(8,128)} %bitcast.1, f32[96,256]{1,0:T(8,128)} %ancestral.1), custom_call_target="tpu_custom_call" | custom-call | tf_op jit(solution)/shard_map/pallas_call | solution.py:339
  33.0 1.3 %copy.8 = f32[16,256]{1,0:T(8,128)} copy(f32[16,256]{1,0:T(8,128)} %shard_map.64) | data formatting | bytes 32768

commit v3 on v2

v3 whole, which is shorter than its diff:
```python
import jax
import jax.numpy as jnp
from jax import lax
from jax.experimental import pallas as pl
from jax.experimental.pallas import tpu as pltpu
from jax.sharding import PartitionSpec as P

branch_one = 0.00025
branch_two = 0.0004
MESH = pl.DeviceIdType.MESH
HIGH = lax.Precision.HIGHEST
F32 = jnp.float32


def device(y, xh, z, xl, c):
    return ((y * 2 + xh) * 8 + z, xl * 2 + c)


def prepared(rows, count, branch):
    order = lax.broadcasted_iota(jnp.int32, rows.shape, 0).astype(F32)
    entry = lax.broadcasted_iota(jnp.int32, rows.shape, 1)
    decay = jnp.exp(-branch * order * (order + 1.0) / 2.0)
    return jnp.where(entry <= count, rows, 0.0) * decay


def kernel(
    slab, counts, rows_one, rows_two, merge, ancestral, out,
    slab_v, one_v, two_v, merge_v, anc_v, anc_pad, one_b, half_v, weights, whi, part, from_core,
    arrived_y, arrived_x, tiles_out, pieces, stack,
    load_sem, slab_sem, merge_sem, core_send, core_recv, y_send, y_recv, x_send, x_recv,
    final_send, final_recv, entered,
):
    pop, mrg = lax.axis_index("pop"), lax.axis_index("merge")
    z = pop % 8
    xh = (pop // 8) % 2
    y = pop // 16
    xl, c = mrg // 2, mrg % 2
    zh = z // 2
    bits_yh, bits_yl = (y // 2, 1 - y // 2), (y % 2, 1 - y % 2)
    bits_xh, bits_xl = (xh, 1 - xh), (xl, 1 - xl)
    bits_zl, bits_c = (z % 2, 1 - z % 2), (c, 1 - c)
    ys = [bits_yh[k // 2] * 2 + bits_yl[k % 2] for k in range(4)]

    barrier = pltpu.get_barrier_semaphore()

    def tell(sem, dev):
        pl.semaphore_signal(sem, inc=1, device_id=dev, device_id_type=MESH)

    for k in (4, 3, 5, 2, 6, 1, 7):
        tell(barrier, device(y, xh, (z + k) % 8, xl, c))
    for k in (2, 3, 1):
        tell(barrier, device(ys[k], xh, z, xl, 1 - c))
        tell(barrier, device(y, bits_xh[k // 2], z, bits_xl[k % 2], 1 - c))
    tell(barrier, device(y, xh, z, 1 - xl, c))
    tell(barrier, device(y, xh, z, xl, 1 - c))

    def y_target(i):
        k = (i % 4 + 1) % 4
        return k, ys[k], bits_xh[1 - i // 4]

    def x_target(i):
        k = i % 4
        xr = 1 - k % 2
        u = (i // 4) * 2 + k // 2
        return u, bits_yh[1 - i // 4] * 2 + bits_yl[k // 2], xr

    def slab_copy(i, h):
        if h == 0:
            _, ty, tx = y_target(i)
            pair = ty * 4 + tx * 2
        else:
            _, ty, xr = x_target(i)
            pair = ty * 4 + bits_xh[xr] * 2 + 1
        begin = pl.multiple_of(pair * 256, 256)
        return pltpu.make_async_copy(
            slab.at[:, :, pl.ds(begin, 256)],
            slab_v.at[i // 2, :, :, pl.ds((i % 2 * 2 + h) * 256, 256)],
            slab_sem.at[i, h],
        )

    load_one = pltpu.make_async_copy(rows_one, one_v, load_sem.at[0])
    load_two = pltpu.make_async_copy(rows_two, two_v, load_sem.at[1])
    load_anc = [
        pltpu.make_async_copy(
            ancestral.at[:, pl.ds(e * 128, 128)], anc_v.at[e], load_sem.at[2 + e]
        )
        for e in range(2)
    ]
    load_one.start()
    load_two.start()
    merge_loads = [
        pltpu.make_async_copy(
            merge.at[:, pl.ds(b * 4, 4)], merge_v.at[:, pl.ds(b * 4, 4)], merge_sem.at[b]
        )
        for b in range(3)
    ]
    for load in merge_loads:
        load.start()

    for i in range(8):
        slab_copy(i, 0).start()
        slab_copy(i, 1).start()
    for load in load_anc:
        load.start()
    own_piece = (z < 4) | (zh == 2 + xl)

    load_one.wait()
    load_two.wait()
    one = prepared(one_v[...], counts[0], branch_one)
    entry = lax.broadcasted_iota(jnp.int32, one.shape, 1)
    for a in range(4):
        column = jnp.sum(jnp.where(entry == pop * 4 + a, one, 0.0), axis=1, keepdims=True)
        one_b[a] = jnp.broadcast_to(column[:, :, None], (96, 8, 96))
    two = prepared(two_v[...], counts[1], branch_two)
    two = pltpu.roll(two, (256 - mrg * 64) % 256, 1)
    two_t = jnp.transpose(two[:, :128])[:64]
    two_hi = two_t.astype(jnp.bfloat16)
    two_lo = (two_t - two_hi.astype(F32)).astype(jnp.bfloat16)
    half_v[...] = jnp.zeros_like(half_v)
    for b in range(3):
        merge_loads[b].wait()

        def mode_step(mb, acc):
            for s in range(8):
                m = mb * 8 + s
                block = merge_v[m, b * 4 : b * 4 + 4]
                acc = tuple(acc[a] + one_b[a, m][None] * block for a in range(4))
            return acc

        acc = lax.fori_loop(0, 12, mode_step, tuple(jnp.zeros((4, 8, 96), F32) for _ in range(4)))
        for a in range(4):
            half_v[b * 32 : b * 32 + 32, a * 128 : a * 128 + 96] = acc[a].reshape(32, 96)
    half = half_v[...]
    half_hi = half.astype(jnp.bfloat16)
    half_lo = (half - half_hi.astype(F32)).astype(jnp.bfloat16)
    wide = (
        jnp.dot(two_hi, half_hi, preferred_element_type=F32)
        + jnp.dot(two_lo, half_hi, preferred_element_type=F32)
        + jnp.dot(two_hi, half_lo, preferred_element_type=F32)
    )
    flat = jnp.concatenate([wide[:, a * 128 : a * 128 + 128] for a in range(4)], axis=0)
    w = jnp.transpose(flat)[:96]
    w_hi = w.astype(jnp.bfloat16)
    weights[:96] = w_hi
    weights[96:] = (w - w_hi.astype(F32)).astype(jnp.bfloat16)
    whi[...] = w_hi

    def core_copy(i, h):
        return pltpu.make_async_remote_copy(
            src_ref=part.at[i, h, 1 - c],
            dst_ref=from_core.at[i, h],
            send_sem=core_send,
            recv_sem=core_recv.at[i, h],
            device_id=device(y, xh, z, xl, 1 - c),
            device_id_type=MESH,
        )

    def contract(b):
        for i in range(2):
            for h in range(2):
                slab_copy(b * 2 + i, h).wait()
        for i in range(2):
            for h in range(2):
                at = (i * 2 + h) * 256
                x = slab_v[b, :, :, at : at + 256].reshape(256, 256)
                x_hi = x.astype(jnp.bfloat16)
                x_lo = (x - x_hi.astype(F32)).astype(jnp.bfloat16)
                both = jnp.dot(weights[...], x_hi, preferred_element_type=F32)
                rest = jnp.dot(whi[...], x_lo, preferred_element_type=F32)
                total = both[:96] + both[96:] + rest
                for j in range(2):
                    for t in range(2):
                        part[b * 2 + i, h, j, t] = total[
                            j * 48 : j * 48 + 48, t * 128 : t * 128 + 128
                        ]

    def swap(b):
        for i in range(2):
            for h in range(2):
                core_copy(b * 2 + i, h).start()

    def forward(i):
        k, ty, _ = y_target(i)
        core_copy(i, 0).wait_recv()
        part[i, 0, c] = part[i, 0, c] + from_core[i, 0]
        pltpu.make_async_remote_copy(
            src_ref=part.at[i, 0, c],
            dst_ref=arrived_y.at[k, i // 4],
            send_sem=y_send,
            recv_sem=y_recv.at[k, i // 4],
            device_id=device(ty, xh, z, xl, 1 - c),
            device_id_type=MESH,
        ).start()

        u, _, xr = x_target(i)
        core_copy(i, 1).wait_recv()
        part[i, 1, c] = part[i, 1, c] + from_core[i, 1]
        for tr in (1, 0):
            pltpu.make_async_remote_copy(
                src_ref=part.at[i, 1, c, bits_xl[tr]],
                dst_ref=arrived_x.at[xr * 2 + tr, u],
                send_sem=x_send,
                recv_sem=x_recv.at[xr * 2 + tr, u],
                device_id=device(y, bits_xh[xr], z, bits_xl[tr], 1 - c),
                device_id_type=MESH,
            ).start()

    contract(0)
    pl.semaphore_wait(barrier, 15)
    tell(entered, device(y, xh, z, 1 - xl, c))
    tell(entered, device(y, xh, z, 1 - xl, 1 - c))
    swap(0)
    contract(1)
    swap(1)
    contract(2)
    swap(2)
    pl.semaphore_wait(entered, 2)
    forward(0)
    forward(1)
    contract(3)
    swap(3)
    for i in range(2, 8):
        forward(i)

    for load in load_anc:
        load.wait()
    anc_pad[...] = jnp.zeros_like(anc_pad)
    stack[...] = jnp.zeros_like(stack)
    for js in range(8):
        for half in range(2):
            at = js * 16 + half * 8
            for e in range(2):
                anc_pad[at : at + 6, e * 128 : e * 128 + 128] = anc_v[
                    e, pl.ds(half * 48 + js, 6, stride=8), :
                ]

    row = lax.broadcasted_iota(jnp.int32, (6, 8, 128), 1)
    group = lax.broadcasted_iota(jnp.int32, (6, 8, 128), 2) // 16

    def spread(total, n, h):
        x = total.reshape(6, 8, 128)
        for b in (1, 2, 4):
            odd_row, odd_group = row // b % 2 == 1, group // b % 2 == 1
            above = pltpu.roll(pltpu.roll(x, 8 - b, 1), 16 * b, 2)
            below = pltpu.roll(pltpu.roll(x, b, 1), 128 - 16 * b, 2)
            x = jnp.where(odd_row == odd_group, x, jnp.where(odd_group, above, below))
        for j in range(6):
            tiles_out[h, n, pl.ds(j, 8, stride=8), :] = x[j]

    def send_pieces(n, h, slot, ty, txh, tzh, own):
        for r in range(8):
            gz, gx, gc = bits_zl[r // 4], bits_xl[r // 2 % 2], bits_c[r % 2]
            begin = pl.multiple_of(gz * 32 + gx * 16 + gc * 8, 8)
            send = pltpu.make_async_remote_copy(
                src_ref=tiles_out.at[h, n, pl.ds(begin, 6), :],
                dst_ref=pieces.at[slot, pl.ds(0, 6), :],
                send_sem=final_send,
                recv_sem=final_recv,
                device_id=device(ty, txh, tzh * 2 + gz, gx, gc),
                device_id_type=MESH,
            )
            if r == 0 and own is not None:

                @pl.when(own)
                def _():
                    pieces[slot, 0:6] = tiles_out[h, n, pl.ds(begin, 6), :]

                @pl.when(jnp.logical_not(own))
                def _():
                    send.start()
            else:
                send.start()

    slot_y = (xh * 2 + xl) * 16 + z * 2 + c
    slot_x = y * 16 + z * 2 + c
    for n in range(4):
        q, t = n // 2, n % 2
        for k in range(4):
            if t == 0:
                pltpu.make_async_copy(
                    arrived_y.at[k, q], arrived_y.at[k, q], y_recv.at[k, q]
                ).wait()
            pltpu.make_async_copy(
                arrived_x.at[k, n], arrived_x.at[k, n], x_recv.at[k, n]
            ).wait()
        spread(
            (arrived_y[0, q, t] + arrived_y[1, q, t]) + (arrived_y[2, q, t] + arrived_y[3, q, t]),
            n,
            0,
        )
        spread((arrived_x[0, n] + arrived_x[1, n]) + (arrived_x[2, n] + arrived_x[3, n]), n, 1)
        send_pieces(n, 0, slot_y, y, bits_xh[1 - q], t, zh == t if q == 1 else None)
        ty = bits_yh[1 - q] * 2 + bits_yl[t]
        send_pieces(n, 1, slot_x, ty, xh, 2 + xl, zh == 2 + xl if n == 2 else None)

    def drain(ref, sem):
        pltpu.make_async_copy(ref, ref, sem).wait()

    def drain_pieces(sem):
        @pl.when(own_piece)
        def _():
            drain(pieces.at[pl.ds(0, 63), pl.ds(0, 6), :], sem)

        @pl.when(jnp.logical_not(own_piece))
        def _():
            drain(pieces.at[:, pl.ds(0, 6), :], sem)

    drain_pieces(final_recv)

    upper, lower = pieces[0, 0:6], pieces[1, 0:6]
    for i in range(1, 32):
        upper = upper + pieces[i * 2, 0:6]
        lower = lower + pieces[i * 2 + 1, 0:6]
    stack[0:6] = lower
    stack[8:14] = upper
    turned = jnp.transpose(stack[...])
    left = turned[0:16]
    for js in range(1, 8):
        left = left + pltpu.roll(turned[js * 16 : js * 16 + 16], js * 16, 1)
    out[...] = jnp.dot(left, anc_pad[...], precision=HIGH, preferred_element_type=F32)

    drain(from_core, core_send)
    drain(arrived_y, y_send)
    drain(arrived_x, x_send)
    drain_pieces(final_send)


def on_device(slab, sample_counts, mode_rows_one, mode_rows_two, merge_tensor, ancestral_modes):
    hbm = pl.BlockSpec(memory_space=pl.ANY)
    dma = pltpu.SemaphoreType.DMA
    return pl.pallas_call(
        kernel,
        out_shape=pltpu.VMEM((16, 256), F32),
        in_specs=[hbm, pl.BlockSpec(memory_space=pltpu.SMEM), hbm, hbm, hbm, hbm],
        out_specs=pl.BlockSpec(memory_space=pltpu.VMEM),
        scratch_shapes=[
            pltpu.VMEM((4, 4, 64, 1024), F32),
            pltpu.VMEM((96, 256), F32),
            pltpu.VMEM((96, 256), F32),
            pltpu.VMEM((96, 12, 8, 96), F32),
            pltpu.VMEM((2, 96, 128), F32),
            pltpu.VMEM((128, 256), F32),
            pltpu.VMEM((4, 96, 8, 96), F32),
            pltpu.VMEM((96, 512), F32),
            pltpu.VMEM((192, 256), jnp.bfloat16),
            pltpu.VMEM((96, 256), jnp.bfloat16),
            pltpu.VMEM((8, 2, 2, 2, 48, 128), F32),
            pltpu.VMEM((8, 2, 2, 48, 128), F32),
            pltpu.VMEM((4, 2, 2, 48, 128), F32),
            pltpu.VMEM((4, 4, 48, 128), F32),
            pltpu.VMEM((2, 4, 64, 128), F32),
            pltpu.VMEM((64, 8, 128), F32),
            pltpu.VMEM((128, 128), F32),
            dma((4,)),
            dma((8, 2)),
            dma((3,)),
            dma,
            dma((8, 2)),
            dma,
            dma((4, 2)),
            dma,
            dma((4, 4)),
            dma,
            dma,
            pltpu.SemaphoreType.REGULAR,
        ],
        compiler_params=pltpu.CompilerParams(
            collective_id=0, has_side_effects=True, vmem_limit_bytes=56 << 20
        ),
    )(
        slab,
        sample_counts,
        mode_rows_one,
        mode_rows_two,
        merge_tensor.reshape(96, 12, 8, 96),
        ancestral_modes,
    )


def solution(mesh):
    in_specs = (P("pop", "merge", None), P(), P(), P(), P(), P())
    out_specs = P(("pop", "merge"), None)
    return jax.shard_map(
        on_device, mesh=mesh, in_specs=in_specs, out_specs=out_specs, check_vma=False
    )
```

time: 34.5 us -> 31.6 us (0.916)
  Pallas kernels: 33 us -> 30.9 us
  local copies, waits for them, and re-layouts: 1.32 us -> 0.61 us
    pallas_call x1, Pallas kernels: 33 us -> 30.9 us  [on_device(): pl.pallas_call(kernel, out_shape=pltpu.VMEM((16, 256), F32), in_specs=[hb...]
    unnamed x1, local copies, waits for them, and re-layouts: 1.32 us -> 0.61 us
where the time goes in v3:
time: 31.6 us; the launch traced here: 31.5 us
  Pallas kernels  30.9 us (98%)
  local copies, waits for them, and re-layouts  0.61 us (2%)
    pallas_call x1, Pallas kernels, on_device(): pl.pallas_call(kernel, out_shape=pltpu.VMEM((16, 256), F32), in_specs=[hb...  30.9 us

profile of v3, /device:TPU:1, one launch (start us, length us, event | category | flops | bytes accessed | tf_op | source)
XLA Modules:
  0.0 31.5 jit_solution(7930429008750950991)
XLA Ops:
  0.0 30.9 %shard_map.64 = f32[16,256]{1,0:T(8,128)S(1)} custom-call(f32[4,64,4096]{2,1,0:T(8,128)} %slab.1, s32[2]{0:T(128)} %counts.1, f32[96,256]{1,0:T(8,128)} %rows_one.1, f32[96,256]{1,0:T(8,128)} %rows_two.1, f32[96,12,8,96]{3,2,1,0:T(8,128)} %bitcast.1, f32[96,256]{1,0:T(8,128)} %ancestral.1), custom_call_target="tpu_custom_call" | custom-call | tf_op jit(solution)/shard_map/pallas_call | solution.py:331
  30.9 0.6 %copy.8 = f32[16,256]{1,0:T(8,128)} copy(f32[16,256]{1,0:T(8,128)S(1)} %shard_map.64) | data formatting | bytes 32768

commit v4 on v3

--- a/solution.py
+++ b/solution.py
@@ -51,7 +51,6 @@
     for k in (2, 3, 1):
         tell(barrier, device(ys[k], xh, z, xl, 1 - c))
         tell(barrier, device(y, bits_xh[k // 2], z, bits_xl[k % 2], 1 - c))
-    tell(barrier, device(y, xh, z, 1 - xl, c))
     tell(barrier, device(y, xh, z, xl, 1 - c))
 
     def y_target(i):
@@ -74,7 +73,7 @@
         begin = pl.multiple_of(pair * 256, 256)
         return pltpu.make_async_copy(
             slab.at[:, :, pl.ds(begin, 256)],
-            slab_v.at[i // 2, :, :, pl.ds((i % 2 * 2 + h) * 256, 256)],
+            slab_v.at[h * 2 + i // 4, :, :, pl.ds(i % 4 * 256, 256)],
             slab_sem.at[i, h],
         )
 
@@ -97,9 +96,9 @@
     for load in merge_loads:
         load.start()
 
-    for i in range(8):
-        slab_copy(i, 0).start()
-        slab_copy(i, 1).start()
+    for h in range(2):
+        for i in range(8):
+            slab_copy(i, h).start()
     for load in load_anc:
         load.start()
     own_piece = (z < 4) | (zh == 2 + xl)
@@ -156,45 +155,43 @@
         )
 
     def contract(b):
-        for i in range(2):
-            for h in range(2):
-                slab_copy(b * 2 + i, h).wait()
-        for i in range(2):
-            for h in range(2):
-                at = (i * 2 + h) * 256
-                x = slab_v[b, :, :, at : at + 256].reshape(256, 256)
-                x_hi = x.astype(jnp.bfloat16)
-                x_lo = (x - x_hi.astype(F32)).astype(jnp.bfloat16)
-                both = jnp.dot(weights[...], x_hi, preferred_element_type=F32)
-                rest = jnp.dot(whi[...], x_lo, preferred_element_type=F32)
-                total = both[:96] + both[96:] + rest
-                for j in range(2):
-                    for t in range(2):
-                        part[b * 2 + i, h, j, t] = total[
-                            j * 48 : j * 48 + 48, t * 128 : t * 128 + 128
-                        ]
+        h, first = b // 2, b % 2 * 4
+        for i in range(4):
+            slab_copy(first + i, h).wait()
+        for i in range(4):
+            x = slab_v[b, :, :, i * 256 : i * 256 + 256].reshape(256, 256)
+            x_hi = x.astype(jnp.bfloat16)
+            x_lo = (x - x_hi.astype(F32)).astype(jnp.bfloat16)
+            both = jnp.dot(weights[...], x_hi, preferred_element_type=F32)
+            rest = jnp.dot(whi[...], x_lo, preferred_element_type=F32)
+            total = both[:96] + both[96:] + rest
+            for j in range(2):
+                for t in range(2):
+                    part[first + i, h, j, t] = total[
+                        j * 48 : j * 48 + 48, t * 128 : t * 128 + 128
+                    ]
 
     def swap(b):
-        for i in range(2):
-            for h in range(2):
-                core_copy(b * 2 + i, h).start()
-
-    def forward(i):
+        for i in range(4):
+            core_copy(b % 2 * 4 + i, b // 2).start()
+
+    def settle(i, h):
+        core_copy(i, h).wait_recv()
+        part[i, h, c] = part[i, h, c] + from_core[i, h]
+
+    def send_y(i, t):
         k, ty, _ = y_target(i)
-        core_copy(i, 0).wait_recv()
-        part[i, 0, c] = part[i, 0, c] + from_core[i, 0]
         pltpu.make_async_remote_copy(
-            src_ref=part.at[i, 0, c],
-            dst_ref=arrived_y.at[k, i // 4],
+            src_ref=part.at[i, 0, c, t],
+            dst_ref=arrived_y.at[k, i // 4, t],
             send_sem=y_send,
-            recv_sem=y_recv.at[k, i // 4],
+            recv_sem=y_recv.at[k, i // 4, t],
             device_id=device(ty, xh, z, xl, 1 - c),
             device_id_type=MESH,
         ).start()
 
+    def send_x(i):
         u, _, xr = x_target(i)
-        core_copy(i, 1).wait_recv()
-        part[i, 1, c] = part[i, 1, c] + from_core[i, 1]
         for tr in (1, 0):
             pltpu.make_async_remote_copy(
                 src_ref=part.at[i, 1, c, bits_xl[tr]],
@@ -206,21 +203,26 @@
             ).start()
 
     contract(0)
-    pl.semaphore_wait(barrier, 15)
-    tell(entered, device(y, xh, z, 1 - xl, c))
-    tell(entered, device(y, xh, z, 1 - xl, 1 - c))
+    pl.semaphore_wait(barrier, 14)
     swap(0)
     contract(1)
     swap(1)
     contract(2)
     swap(2)
-    pl.semaphore_wait(entered, 2)
-    forward(0)
-    forward(1)
+    for i in range(8):
+        settle(i, 0)
+        if i == 0:
+            for k in (2, 3, 1):
+                tell(entered, device(y, bits_xh[k // 2], z, bits_xl[k % 2], 1 - c))
+        send_y(i, 0)
+    pl.semaphore_wait(entered, 3)
+    for i in range(8):
+        send_y(i, 1)
     contract(3)
     swap(3)
-    for i in range(2, 8):
-        forward(i)
+    for i in range(8):
+        settle(i, 1)
+        send_x(i)
 
     for load in load_anc:
         load.wait()
@@ -247,9 +249,9 @@
         for j in range(6):
             tiles_out[h, n, pl.ds(j, 8, stride=8), :] = x[j]
 
-    def send_pieces(n, h, slot, ty, txh, tzh, own):
+    def send_pieces(n, h, slot, ty, txh, tzh, own, near):
         for r in range(8):
-            gz, gx, gc = bits_zl[r // 4], bits_xl[r // 2 % 2], bits_c[r % 2]
+            gz, gx, gc = near + r // 4 * (1 - 2 * near), bits_xl[r // 2 % 2], bits_c[r % 2]
             begin = pl.multiple_of(gz * 32 + gx * 16 + gc * 8, 8)
             send = pltpu.make_async_remote_copy(
                 src_ref=tiles_out.at[h, n, pl.ds(begin, 6), :],
@@ -259,13 +261,14 @@
                 device_id=device(ty, txh, tzh * 2 + gz, gx, gc),
                 device_id_type=MESH,
             )
-            if r == 0 and own is not None:
-
-                @pl.when(own)
+            if r % 4 == 0 and own is not None:
+                mine = own & (z % 2 == gz)
+
+                @pl.when(mine)
                 def _():
                     pieces[slot, 0:6] = tiles_out[h, n, pl.ds(begin, 6), :]
 
-                @pl.when(jnp.logical_not(own))
+                @pl.when(jnp.logical_not(mine))
                 def _():
                     send.start()
             else:
@@ -273,25 +276,27 @@
 
     slot_y = (xh * 2 + xl) * 16 + z * 2 + c
     slot_x = y * 16 + z * 2 + c
-    for n in range(4):
+    for n in (0, 2, 1, 3):
         q, t = n // 2, n % 2
         for k in range(4):
-            if t == 0:
-                pltpu.make_async_copy(
-                    arrived_y.at[k, q], arrived_y.at[k, q], y_recv.at[k, q]
-                ).wait()
             pltpu.make_async_copy(
-                arrived_x.at[k, n], arrived_x.at[k, n], x_recv.at[k, n]
+                arrived_y.at[k, q, t], arrived_y.at[k, q, t], y_recv.at[k, q, t]
             ).wait()
         spread(
             (arrived_y[0, q, t] + arrived_y[1, q, t]) + (arrived_y[2, q, t] + arrived_y[3, q, t]),
             n,
             0,
         )
+        send_pieces(n, 0, slot_y, y, bits_xh[1 - q], t, zh == t if q == 1 else None, t)
+    for n in range(4):
+        q, t = n // 2, n % 2
+        for k in range(4):
+            pltpu.make_async_copy(
+                arrived_x.at[k, n], arrived_x.at[k, n], x_recv.at[k, n]
+            ).wait()
         spread((arrived_x[0, n] + arrived_x[1, n]) + (arrived_x[2, n] + arrived_x[3, n]), n, 1)
-        send_pieces(n, 0, slot_y, y, bits_xh[1 - q], t, zh == t if q == 1 else None)
         ty = bits_yh[1 - q] * 2 + bits_yl[t]
-        send_pieces(n, 1, slot_x, ty, xh, 2 + xl, zh == 2 + xl if n == 2 else None)
+        send_pieces(n, 1, slot_x, ty, xh, 2 + xl, zh == 2 + xl if n == 2 else None, 0)
 
     def drain(ref, sem):
         pltpu.make_async_copy(ref, ref, sem).wait()
@@ -357,7 +362,7 @@
             dma,
             dma((8, 2)),
             dma,
-            dma((4, 2)),
+            dma((4, 2, 2)),
             dma,
             dma((4, 4)),
             dma,

time: 31.6 us -> 27.4 us (0.87)
  the two profiles are of different devices: /device:TPU:1 before, /device:TPU:99 now
where the time goes in v4:
time: 27.4 us
  Pallas kernels  26.7 us (97%)
  local copies, waits for them, and re-layouts  0.61 us (2%)
    pallas_call x1, Pallas kernels, on_device(): pl.pallas_call(kernel, out_shape=pltpu.VMEM((16, 256), F32), in_specs=[hb...  26.7 us
    unnamed x1, local copies, waits for them, and re-layouts  0.61 us

profile of v4, /device:TPU:99, one launch (start us, length us, event | category | flops | bytes accessed | tf_op | source)
XLA Modules:
  0.0 27.4 jit_solution(16128712654019714733)
XLA Ops:
  0.0 26.7 %shard_map.64 = f32[16,256]{1,0:T(8,128)S(1)} custom-call(f32[4,64,4096]{2,1,0:T(8,128)} %slab.1, s32[2]{0:T(128)} %counts.1, f32[96,256]{1,0:T(8,128)} %rows_one.1, f32[96,256]{1,0:T(8,128)} %rows_two.1, f32[96,12,8,96]{3,2,1,0:T(8,128)} %bitcast.1, f32[96,256]{1,0:T(8,128)} %ancestral.1), custom_call_target="tpu_custom_call" | custom-call | tf_op jit(solution)/shard_map/pallas_call | solution.py:336
  26.7 0.6 %copy.8 = f32[16,256]{1,0:T(8,128)} copy(f32[16,256]{1,0:T(8,128)S(1)} %shard_map.64) | data formatting | bytes 32768

commit v5 on v4

--- a/solution.py
+++ b/solution.py
@@ -28,7 +28,7 @@
     slab_v, one_v, two_v, merge_v, anc_v, anc_pad, one_b, half_v, weights, whi, part, from_core,
     arrived_y, arrived_x, tiles_out, pieces, stack,
     load_sem, slab_sem, merge_sem, core_send, core_recv, y_send, y_recv, x_send, x_recv,
-    final_send, final_recv, entered,
+    final_send, final_recv, entered_near, entered_far,
 ):
     pop, mrg = lax.axis_index("pop"), lax.axis_index("merge")
     z = pop % 8
@@ -46,22 +46,15 @@
     def tell(sem, dev):
         pl.semaphore_signal(sem, inc=1, device_id=dev, device_id_type=MESH)
 
-    for k in (4, 3, 5, 2, 6, 1, 7):
-        tell(barrier, device(y, xh, (z + k) % 8, xl, c))
-    for k in (2, 3, 1):
-        tell(barrier, device(ys[k], xh, z, xl, 1 - c))
-        tell(barrier, device(y, bits_xh[k // 2], z, bits_xl[k % 2], 1 - c))
-    tell(barrier, device(y, xh, z, xl, 1 - c))
 
     def y_target(i):
-        k = (i % 4 + 1) % 4
-        return k, ys[k], bits_xh[1 - i // 4]
+        return y, i % 4, bits_xh[1 - i // 4]
 
     def x_target(i):
         k = i % 4
         xr = 1 - k % 2
         u = (i // 4) * 2 + k // 2
-        return u, bits_yh[1 - i // 4] * 2 + bits_yl[k // 2], xr
+        return u, u, xr
 
     def slab_copy(i, h):
         if h == 0:
@@ -96,6 +89,13 @@
     for load in merge_loads:
         load.start()
 
+    for k in (4, 3, 5, 2, 6, 1, 7):
+        tell(barrier, device(y, xh, (z + k) % 8, xl, c))
+    for k in (2, 3, 1):
+        tell(barrier, device(ys[k], xh, z, xl, 1 - c))
+        for core in range(2):
+            tell(barrier, device(y, bits_xh[k // 2], z, bits_xl[k % 2], core))
+    tell(barrier, device(y, xh, z, xl, 1 - c))
     for h in range(2):
         for i in range(8):
             slab_copy(i, h).start()
@@ -154,22 +154,26 @@
             device_id_type=MESH,
         )
 
+    def contract_pair(b, i):
+        h, at = b // 2, b % 2 * 4 + i
+        x = slab_v[b, :, :, i * 256 : i * 256 + 256].reshape(256, 256)
+        x_hi = x.astype(jnp.bfloat16)
+        x_lo = (x - x_hi.astype(F32)).astype(jnp.bfloat16)
+        both = jnp.dot(weights[...], x_hi, preferred_element_type=F32)
+        rest = jnp.dot(whi[...], x_lo, preferred_element_type=F32)
+        total = both[:96] + both[96:] + rest
+        for j in range(2):
+            for t in range(2):
+                part[at, h, j, t] = total[j * 48 : j * 48 + 48, t * 128 : t * 128 + 128]
+
+    def arrive(b):
+        for i in range(4):
+            slab_copy(b % 2 * 4 + i, b // 2).wait()
+
     def contract(b):
-        h, first = b // 2, b % 2 * 4
+        arrive(b)
         for i in range(4):
-            slab_copy(first + i, h).wait()
-        for i in range(4):
-            x = slab_v[b, :, :, i * 256 : i * 256 + 256].reshape(256, 256)
-            x_hi = x.astype(jnp.bfloat16)
-            x_lo = (x - x_hi.astype(F32)).astype(jnp.bfloat16)
-            both = jnp.dot(weights[...], x_hi, preferred_element_type=F32)
-            rest = jnp.dot(whi[...], x_lo, preferred_element_type=F32)
-            total = both[:96] + both[96:] + rest
-            for j in range(2):
-                for t in range(2):
-                    part[first + i, h, j, t] = total[
-                        j * 48 : j * 48 + 48, t * 128 : t * 128 + 128
-                    ]
+            contract_pair(b, i)
 
     def swap(b):
         for i in range(4):
@@ -202,27 +206,38 @@
                 device_id_type=MESH,
             ).start()
 
-    contract(0)
-    pl.semaphore_wait(barrier, 14)
-    swap(0)
+    arrive(0)
+    contract_pair(0, 0)
+    pl.semaphore_wait(barrier, 17)
+    for core in range(2):
+        tell(entered_near, device(y, xh, z, 1 - xl, core))
+    for k in (2, 3):
+        for core in range(2):
+            tell(entered_far, device(y, 1 - xh, z, bits_xl[k % 2], core))
+    core_copy(0, 0).start()
+    for i in range(1, 4):
+        contract_pair(0, i)
+        core_copy(i, 0).start()
     contract(1)
     swap(1)
+    for i in range(8):
+        settle(i, 0)
+        if i == 4:
+            pl.semaphore_wait(entered_near, 2)
+        send_y(i, 0)
     contract(2)
     swap(2)
-    for i in range(8):
-        settle(i, 0)
-        if i == 0:
-            for k in (2, 3, 1):
-                tell(entered, device(y, bits_xh[k // 2], z, bits_xl[k % 2], 1 - c))
-        send_y(i, 0)
-    pl.semaphore_wait(entered, 3)
+    contract(3)
+    swap(3)
+    for i in range(4):
+        settle(i, 1)
+        send_x(i)
     for i in range(8):
         send_y(i, 1)
-    contract(3)
-    swap(3)
-    for i in range(8):
+    for i in range(4, 8):
         settle(i, 1)
         send_x(i)
+    pl.semaphore_wait(entered_far, 4)
 
     for load in load_anc:
         load.wait()
@@ -276,7 +291,7 @@
 
     slot_y = (xh * 2 + xl) * 16 + z * 2 + c
     slot_x = y * 16 + z * 2 + c
-    for n in (0, 2, 1, 3):
+    def deliver_y(n):
         q, t = n // 2, n % 2
         for k in range(4):
             pltpu.make_async_copy(
@@ -288,15 +303,24 @@
             0,
         )
         send_pieces(n, 0, slot_y, y, bits_xh[1 - q], t, zh == t if q == 1 else None, t)
-    for n in range(4):
+
+    def deliver_x(n):
         q, t = n // 2, n % 2
         for k in range(4):
             pltpu.make_async_copy(
                 arrived_x.at[k, n], arrived_x.at[k, n], x_recv.at[k, n]
             ).wait()
         spread((arrived_x[0, n] + arrived_x[1, n]) + (arrived_x[2, n] + arrived_x[3, n]), n, 1)
-        ty = bits_yh[1 - q] * 2 + bits_yl[t]
-        send_pieces(n, 1, slot_x, ty, xh, 2 + xl, zh == 2 + xl if n == 2 else None, 0)
+        send_pieces(n, 1, slot_x, n, xh, 2 + xl, (zh == 2 + xl) & (y == n), 0)
+
+    deliver_y(0)
+    deliver_y(2)
+    deliver_y(1)
+    deliver_y(3)
+    deliver_x(0)
+    deliver_x(1)
+    deliver_x(2)
+    deliver_x(3)
 
     def drain(ref, sem):
         pltpu.make_async_copy(ref, ref, sem).wait()
@@ -368,6 +392,7 @@
             dma,
             dma,
             pltpu.SemaphoreType.REGULAR,
+            pltpu.SemaphoreType.REGULAR,
         ],
         compiler_params=pltpu.CompilerParams(
             collective_id=0, has_side_effects=True, vmem_limit_bytes=56 << 20

time: 27.4 us -> 26.1 us (0.953)
  the two profiles are of different devices: /device:TPU:99 before, /device:TPU:98 now
where the time goes in v5:
time: 26.1 us; the launch traced here: 26 us
  Pallas kernels  25.4 us (97%)
  local copies, waits for them, and re-layouts  0.61 us (2%)
    pallas_call x1, Pallas kernels, on_device(): pl.pallas_call(kernel, out_shape=pltpu.VMEM((16, 256), F32), in_specs=[hb...  25.4 us
    unnamed x1, local copies, waits for them, and re-layouts  0.61 us

profile of v5, /device:TPU:98, one launch (start us, length us, event | category | flops | bytes accessed | tf_op | source)
XLA Modules:
  0.0 26.0 jit_solution(1590695444124572697)
XLA Ops:
  0.0 25.4 %shard_map.64 = f32[16,256]{1,0:T(8,128)S(1)} custom-call(f32[4,64,4096]{2,1,0:T(8,128)} %slab.1, s32[2]{0:T(128)} %counts.1, f32[96,256]{1,0:T(8,128)} %rows_one.1, f32[96,256]{1,0:T(8,128)} %rows_two.1, f32[96,12,8,96]{3,2,1,0:T(8,128)} %bitcast.1, f32[96,256]{1,0:T(8,128)} %ancestral.1), custom_call_target="tpu_custom_call" | custom-call | tf_op jit(solution)/shard_map/pallas_call | solution.py:360
  25.4 0.6 %copy.8 = f32[16,256]{1,0:T(8,128)} copy(f32[16,256]{1,0:T(8,128)S(1)} %shard_map.64) | data formatting | bytes 32768

commit v6 on v5

--- a/solution.py
+++ b/solution.py
@@ -264,9 +264,9 @@
         for j in range(6):
             tiles_out[h, n, pl.ds(j, 8, stride=8), :] = x[j]
 
-    def send_pieces(n, h, slot, ty, txh, tzh, own, near):
-        for r in range(8):
-            gz, gx, gc = near + r // 4 * (1 - 2 * near), bits_xl[r // 2 % 2], bits_c[r % 2]
+    def send_pieces(n, h, slot, ty, txh, tzh, own, gz):
+        for r in range(4):
+            gx, gc = bits_xl[r // 2], bits_c[r % 2]
             begin = pl.multiple_of(gz * 32 + gx * 16 + gc * 8, 8)
             send = pltpu.make_async_remote_copy(
                 src_ref=tiles_out.at[h, n, pl.ds(begin, 6), :],
@@ -276,7 +276,7 @@
                 device_id=device(ty, txh, tzh * 2 + gz, gx, gc),
                 device_id_type=MESH,
             )
-            if r % 4 == 0 and own is not None:
+            if r == 0 and own is not None:
                 mine = own & (z % 2 == gz)
 
                 @pl.when(mine)
@@ -302,7 +302,10 @@
             n,
             0,
         )
-        send_pieces(n, 0, slot_y, y, bits_xh[1 - q], t, zh == t if q == 1 else None, t)
+
+    def send_z(n, gz):
+        q, t = n // 2, n % 2
+        send_pieces(n, 0, slot_y, y, bits_xh[1 - q], t, zh == t if q == 1 else None, gz)
 
     def deliver_x(n):
         q, t = n // 2, n % 2
@@ -311,12 +314,21 @@
                 arrived_x.at[k, n], arrived_x.at[k, n], x_recv.at[k, n]
             ).wait()
         spread((arrived_x[0, n] + arrived_x[1, n]) + (arrived_x[2, n] + arrived_x[3, n]), n, 1)
-        send_pieces(n, 1, slot_x, n, xh, 2 + xl, (zh == 2 + xl) & (y == n), 0)
+        for gz in (1, 0):
+            send_pieces(n, 1, slot_x, n, xh, 2 + xl, (zh == 2 + xl) & (y == n), gz)
 
     deliver_y(0)
+    send_z(0, 0)
+    send_z(0, 1)
     deliver_y(2)
+    send_z(2, 0)
+    send_z(2, 1)
     deliver_y(1)
+    send_z(1, 1)
+    send_z(1, 0)
     deliver_y(3)
+    send_z(3, 1)
+    send_z(3, 0)
     deliver_x(0)
     deliver_x(1)
     deliver_x(2)

time: 26.1 us -> 26.1 us (level)
  no operation moved by 1% of the time
where the time goes in v6:
time: 26.1 us; the launch traced here: 26 us
  Pallas kernels  25.4 us (97%)
  local copies, waits for them, and re-layouts  0.61 us (2%)
    pallas_call x1, Pallas kernels, on_device(): pl.pallas_call(kernel, out_shape=pltpu.VMEM((16, 256), F32), in_specs=[hb...  25.4 us
    unnamed x1, local copies, waits for them, and re-layouts  0.61 us

profile of v6, /device:TPU:98, one launch (start us, length us, event | category | flops | bytes accessed | tf_op | source)
XLA Modules:
  0.0 26.0 jit_solution(11896694481573466525)
XLA Ops:
  0.0 25.4 %shard_map.64 = f32[16,256]{1,0:T(8,128)S(1)} custom-call(f32[4,64,4096]{2,1,0:T(8,128)} %slab.1, s32[2]{0:T(128)} %counts.1, f32[96,256]{1,0:T(8,128)} %rows_one.1, f32[96,256]{1,0:T(8,128)} %rows_two.1, f32[96,12,8,96]{3,2,1,0:T(8,128)} %bitcast.1, f32[96,256]{1,0:T(8,128)} %ancestral.1), custom_call_target="tpu_custom_call" | custom-call | tf_op jit(solution)/shard_map/pallas_call | solution.py:372
  25.4 0.6 %copy.8 = f32[16,256]{1,0:T(8,128)} copy(f32[16,256]{1,0:T(8,128)S(1)} %shard_map.64) | data formatting | bytes 32768

commit v7 on v5

--- a/solution.py
+++ b/solution.py
@@ -225,6 +225,8 @@
         if i == 4:
             pl.semaphore_wait(entered_near, 2)
         send_y(i, 0)
+    for i in range(8):
+        send_y(i, 1)
     contract(2)
     swap(2)
     contract(3)
@@ -232,8 +234,6 @@
     for i in range(4):
         settle(i, 1)
         send_x(i)
-    for i in range(8):
-        send_y(i, 1)
     for i in range(4, 8):
         settle(i, 1)
         send_x(i)

time: 26.1 us -> 26.7 us (1.023)
  the two profiles are of different devices: /device:TPU:98 before, /device:TPU:103 now
where the time goes in v7:
time: 26.7 us; the launch traced here: 26.6 us
  Pallas kernels  26 us (97%)
  local copies, waits for them, and re-layouts  0.61 us (2%)
    pallas_call x1, Pallas kernels, on_device(): pl.pallas_call(kernel, out_shape=pltpu.VMEM((16, 256), F32), in_specs=[hb...  26 us
    unnamed x1, local copies, waits for them, and re-layouts  0.61 us

profile of v7, /device:TPU:103, one launch (start us, length us, event | category | flops | bytes accessed | tf_op | source)
XLA Modules:
  0.0 26.6 jit_solution(11120064239406330965)
XLA Ops:
  0.0 26.0 %shard_map.64 = f32[16,256]{1,0:T(8,128)S(1)} custom-call(f32[4,64,4096]{2,1,0:T(8,128)} %slab.1, s32[2]{0:T(128)} %counts.1, f32[96,256]{1,0:T(8,128)} %rows_one.1, f32[96,256]{1,0:T(8,128)} %rows_two.1, f32[96,12,8,96]{3,2,1,0:T(8,128)} %bitcast.1, f32[96,256]{1,0:T(8,128)} %ancestral.1), custom_call_target="tpu_custom_call" | custom-call | tf_op jit(solution)/shard_map/pallas_call | solution.py:360
  26.0 0.6 %copy.8 = f32[16,256]{1,0:T(8,128)} copy(f32[16,256]{1,0:T(8,128)S(1)} %shard_map.64) | data formatting | bytes 32768
